TPU v7x, 256 devices: a whole 4x4x8 slice. The times are simulated.
256 devices in a mesh: tp: 8 (over y, z_hi), dp: 8 (over z_lo, core), hg: 4 (over x).
Axes of the slice: x: 4, y: 4, z: 8 (z_hi: 2, z_lo: 4; z = z_hi * 4 + z_lo), core: 2. Of those that a mesh axis runs over, the one named last changes fastest.
Arguments:
- hidden_in: bfloat16 [8, 4, 256, 4096], P('dp', 'hg', 'tp'), may hold values from -45 to 45
- norm_gain: float32 [4096], replicated, may hold values from 0.1 to 1.9
- qkv_weight: bfloat16 [4096, 3, 32, 128], P(('dp', 'hg'), None, 'tp'), may hold values from -0.09375 to 0.09375
- out_weight: bfloat16 [32, 128, 4096], P('tp', None, ('dp', 'hg')), may hold values from -0.5 to 0.5
- cache_kv: bfloat16 [8, 32, 1024, 256], P('dp', 'tp'), may hold values from -200 to 200
- cached_lengths: int32 [8], replicated, may hold values from 128 to 1024, as said below
- owner_table: int32 [8, 16], replicated, may hold values from 0 to 7, as said below
Outputs:
- hidden_out: bfloat16 [8, 4, 256, 4096], P('dp', 'hg', 'tp')
- decode_kv: bfloat16 [8, 32, 8, 2, 128, 256], P('dp', ('tp', 'hg'))
Inputs may be any that keep to these rules, and one draw needn't show every extreme that they name: `cached_lengths`: multiples of 128; one request has exactly 1024. `owner_table`: a request has at most 2 valid blocks with one owner; one owner holds exactly 2 valid blocks of every request.
All inputs are finite; a program needn't handle non-finite values.
Results may differ from a plain program's by a relative error of at most 0.015.
Values may be sent and summed in bfloat16 or wider, within the bound.
A program may use at most 128 MiB of HBM per device.

v0:
```python
import math

import jax
import jax.numpy as jnp
from jax import lax
from jax.sharding import PartitionSpec as P

ROT = 32
BLOCK = 128


epsilon = 1e-05


def layer_norm(row_data, gain_row):
    row_data = row_data.astype(jnp.float32)
    centered = row_data - jnp.mean(row_data, axis=-1, keepdims=True)
    spread = jnp.mean(centered * centered, axis=-1, keepdims=True)
    return (centered * lax.rsqrt(spread + epsilon) * gain_row).astype(jnp.bfloat16)


def rotate(vectors, positions, rot_dims):
    half_dims = rot_dims // 2
    frequency = 10000.0 ** (-2.0 * jnp.arange(half_dims, dtype=jnp.float32) / rot_dims)
    angles = positions.astype(jnp.float32)[:, None, None] * frequency[None, None, :]
    cosine = jnp.cos(angles)
    sine_part = jnp.sin(angles)
    first_half = vectors[..., :half_dims]
    second = vectors[..., half_dims:rot_dims]
    return jnp.concatenate(
        [
            first_half * cosine - second * sine_part,
            second * cosine + first_half * sine_part,
            vectors[..., rot_dims:],
        ],
        axis=-1,
    )


def attend(queries, key_rows, value_rows, limit_base):
    scores = jnp.dot(queries, key_rows.T, preferred_element_type=jnp.float32) / math.sqrt(
        queries.shape[-1]
    )
    row_limit = limit_base + jnp.arange(queries.shape[0], dtype=jnp.int32)
    allowed = jnp.arange(key_rows.shape[0], dtype=jnp.int32)[None, :] <= row_limit[:, None]
    scores = jnp.where(allowed, scores, -jnp.inf)
    row_max = jnp.max(scores, axis=1, keepdims=True)
    weights = jnp.exp(scores - row_max)
    row_total = jnp.sum(weights, axis=1, keepdims=True)
    attended = (
        jnp.dot(weights.astype(jnp.bfloat16), value_rows, preferred_element_type=jnp.float32)
        / row_total
    )
    return attended.astype(jnp.bfloat16)


def selector(owner_row, valid_end, low_block, high_block, owner_count, slot_cap):
    block_ids = jnp.arange(owner_row.shape[0], dtype=jnp.int32)
    is_valid = block_ids < valid_end
    same_owner = (
        (owner_row[:, None] == owner_row[None, :])
        & is_valid[None, :]
        & (block_ids[None, :] < block_ids[:, None])
    )
    slot_rank = jnp.sum(same_owner.astype(jnp.int32), axis=1)
    chosen = is_valid & (block_ids >= low_block) & (block_ids < high_block)
    slot_ids = jnp.arange(owner_count * slot_cap, dtype=jnp.int32)
    picked = (
        chosen[None, :]
        & (owner_row[None, :] == (slot_ids // slot_cap)[:, None])
        & (slot_rank[None, :] == (slot_ids % slot_cap)[:, None])
    )
    return picked.astype(jnp.bfloat16)


def on_device(hidden_in, norm_gain, qkv_weight, out_weight, cache_kv, cached_lengths, owner_table):
    tp_count = lax.axis_size("tp")
    run_count = lax.axis_size("hg")
    owner_count = lax.axis_size("dp")
    request = lax.axis_index("dp")
    run_index = lax.axis_index("hg")
    length = lax.dynamic_index_in_dim(cached_lengths, request, 0, keepdims=False)
    owner_row = lax.dynamic_index_in_dim(owner_table, request, 0, keepdims=False)
    local_rows = hidden_in.shape[2]
    run_len = local_rows * tp_count
    stretch_len = run_len * run_count
    model_width = hidden_in.shape[3]
    local_heads = qkv_weight.shape[2]
    head_dim = qkv_weight.shape[3]
    head_width = local_heads * head_dim
    group_heads = local_heads // run_count
    seq_span = cache_kv.shape[2] + stretch_len
    block_count = seq_span // BLOCK
    slot_cap = (block_count + owner_count - 1) // owner_count
    valid_end = (length + stretch_len) // BLOCK
    run_first = run_index * run_len
    zero_index = jnp.zeros((), jnp.int32)
    extended = jnp.concatenate(
        [cache_kv[0], jnp.zeros((local_heads, stretch_len, 2 * head_dim), jnp.bfloat16)], axis=1
    )
    run_rows = lax.all_gather(hidden_in, "tp", axis=2, tiled=True)[0, 0]
    normed = layer_norm(run_rows, norm_gain)
    piece = lax.all_gather(qkv_weight, ("dp", "hg"), axis=0, tiled=True)
    projected = jnp.dot(
        normed, piece.reshape(piece.shape[0], 3 * head_width), preferred_element_type=jnp.float32
    )
    positions = length + run_first + jnp.arange(run_len, dtype=jnp.int32)
    queries = rotate(
        projected[:, :head_width].reshape(run_len, local_heads, head_dim), positions, ROT
    ).astype(jnp.bfloat16)
    new_keys = rotate(
        projected[:, head_width : 2 * head_width].reshape(run_len, local_heads, head_dim),
        positions,
        ROT,
    ).astype(jnp.bfloat16)
    new_values = (
        projected[:, 2 * head_width :].reshape(run_len, local_heads, head_dim).astype(jnp.bfloat16)
    )
    run_kv = jnp.concatenate([new_keys, new_values], axis=2).transpose(1, 0, 2)
    stretch_kv = lax.all_gather(run_kv, "hg", axis=1, tiled=True)

    def one_head(operands):
        head_queries, head_extended, head_stretch = operands
        sequence = lax.dynamic_update_slice(head_extended, head_stretch, (length, zero_index))
        return (
            attend(
                head_queries, sequence[:, :head_dim], sequence[:, head_dim:], length + run_first
            ),
            sequence,
        )

    attended, sequence = lax.map(one_head, (queries.transpose(1, 0, 2), extended, stretch_kv))
    attended_rows = attended.transpose(1, 0, 2).reshape(run_len, head_width)
    out_full = lax.all_gather(out_weight, ("dp", "hg"), axis=2, tiled=True)
    out_flat = out_full.reshape(head_width, model_width)
    reduced = lax.psum_scatter(
        jnp.dot(attended_rows, out_flat, preferred_element_type=jnp.float32).astype(jnp.bfloat16),
        "tp",
        scatter_dimension=0,
        tiled=True,
    ).astype(jnp.float32)
    hidden_out = (hidden_in[0, 0].astype(jnp.float32) + reduced).astype(jnp.bfloat16)[None, None]
    mine = lax.dynamic_slice_in_dim(sequence, run_index * group_heads, group_heads, 0)
    picked = selector(owner_row, valid_end, 0, valid_end, owner_count, slot_cap).reshape(
        owner_count, slot_cap, block_count
    )
    blocks = mine.reshape(group_heads, block_count, BLOCK * 2 * head_dim)
    placed = jnp.einsum("ocb,hbx->ohcx", picked, blocks, preferred_element_type=jnp.float32)
    received = lax.all_to_all(
        placed.astype(jnp.bfloat16).reshape(
            owner_count, group_heads, 1, slot_cap, BLOCK, 2 * head_dim
        ),
        "dp",
        split_axis=0,
        concat_axis=2,
        tiled=True,
    )
    return (hidden_out, received)


def solution(mesh):
    return jax.shard_map(
        on_device,
        mesh=mesh,
        in_specs=(
            P("dp", "hg", "tp", None),
            P(),
            P(("dp", "hg"), None, "tp", None),
            P("tp", None, ("dp", "hg")),
            P("dp", "tp", None, None),
            P(),
            P(),
        ),
        out_specs=(P("dp", "hg", "tp", None), P("dp", ("tp", "hg"), None, None, None, None)),
        check_vma=False,
    )
```

profile of v0, /device:TPU:3, one launch (start us, length us, event | category | flops | bytes accessed | tf_op | source)
XLA Modules:
  0.0 447.7 jit_solution(7063650462905624844)
XLA Ops:
  8.7 1.2 dynamic_slice.29
  11.5 70.9 %all-gather.5.cloned.1.call-done = bf16[1,1,256,4096]{3,2,1,0:T(8,128)(2,1)} async-done(((bf16[1,1,32,4096]{3,2,1,0:T(8,128)(2,1)}), bf16[1,1,256,4096]{3,2,1,0:T(8,128)(2,1)}) %all-gather.5.cloned.1.call-update) | async-done | bytes 2097168 | tf_op jit(solution)/shard_map/all_gather | solution.py:101
  82.4 2.1 convert_reduce_fusion
  85.4 101.2 %all-gather.7.cloned.1.call-done = bf16[4096,3,4,128]{3,2,1,0:T(4,128)(2,1)} async-done(((bf16[128,3,4,128]{3,2,1,0:T(4,128)(2,1)}), bf16[4096,3,4,128]{3,2,1,0:T(4,128)(2,1)}) %all-gather.7.cloned.1.call-update) | async-done | bytes 12582928 | tf_op jit(solution)/shard_map/all_gather | solution.py:103
  186.5 20.9 %reshape.208 = bf16[4096,1536]{1,0:T(8,128)(2,1)} reshape(bf16[4096,3,4,128]{3,2,1,0:T(4,128)(2,1)} %all-gather.7.cloned.1.call-done) | data formatting | bytes 25165824 | tf_op jit(solution)/shard_map/reshape | solution.py:105
  207.4 6.9 %fusion.21 = f32[256,1536]{1,0:T(8,128)S(1)} fusion(bf16[4096,1536]{1,0:T(8,128)(2,1)} %reshape.208, bf16[1,1,256,4096]{3,2,1,0:T(8,128)(2,1)S(1)} %copy-done.1, f32[4096]{0:T(1024)S(1)} %copy-done.6, f32[256]{0:T(256)S(1)} %add_rsqrt_fusion, f32[256]{0:T(256)S(1)} %broadcast_multiply_fusion), kind=kOutput, calls=%fused_computation.33 | convolution fusion | flops 3226468352 | bytes 16271360 | tf_op jit(solution)/shard_map/dot_general | solution.py:104
  217.0 1.2 maximum_bitcast_fusion
  220.6 2.2 concatenate.14
  223.4 28.0 %all-gather.9.cloned.1.call-done = bf16[4,1024,256]{2,1,0:T(8,128)(2,1)} async-done(((bf16[4,256,256]{2,1,0:T(8,128)(2,1)}), bf16[4,1024,256]{2,1,0:T(8,128)(2,1)}) %all-gather.9.cloned.1.call-update) | async-done | bytes 2097168 | tf_op jit(solution)/shard_map/all_gather | solution.py:120
  251.4 32.4 %while.14 = (s32[]{:T(128)}, bf16[4,256,128]{2,1,0:T(8,128)(2,1)S(1)}, bf16[4,2048,256]{2,1,0:T(8,128)(2,1)}, s32[]{:T(128)}, bf16[4,256,128]{2,1,0:T(8,128)(2,1...) while((s32[]{:T(128)}, ...), condition=%wide.region_5.6_spmd, body=%wide.region_2.5_spmd.sunk | while | flops 272695040 | bytes 13769865 | solution.py:132
  251.4 1.1 dynamic-slice_bitcast_fusion.6
  252.4 1.3 dynamic-slice_bitcast_fusion.5
  253.7 3.0 dynamic_update_slice.24
  258.4 1.1 bitcast_dynamic-update-slice_fusion.2
  259.5 1.1 dynamic-slice_bitcast_fusion.6
  260.6 1.3 dynamic-slice_bitcast_fusion.5
  261.9 3.0 dynamic_update_slice.24
  266.5 1.0 bitcast_dynamic-update-slice_fusion.2
  267.5 1.1 dynamic-slice_bitcast_fusion.6
  268.6 1.3 dynamic-slice_bitcast_fusion.5
  269.9 3.0 dynamic_update_slice.24
  274.5 1.1 bitcast_dynamic-update-slice_fusion.2
  275.6 1.1 dynamic-slice_bitcast_fusion.6
  276.7 1.3 dynamic-slice_bitcast_fusion.5
  278.0 3.0 dynamic_update_slice.24
  282.6 1.1 bitcast_dynamic-update-slice_fusion.2
  283.7 56.0 %all-gather.11.cloned.1.call-done = bf16[4,128,4096]{2,1,0:T(8,128)(2,1)} async-done(((bf16[4,128,128]{2,1,0:T(8,128)(2,1)}), bf16[4,128,4096]{2,1,0:T(8,128)(2,1)}) %all-gather.11.cloned.1.call-update) | async-done | bytes 4194320 | tf_op jit(solution)/shard_map/all_gather | solution.py:134
  339.7 4.8 %fusion.13 = bf16[256,4096]{1,0:T(8,128)(2,1)} fusion(bf16[4,128,4096]{2,1,0:T(8,128)(2,1)} %all-gather.11.cloned.1.call-done, bf16[4,256,128]{2,1,0:T(8,128)(2,1)S(1)} %get-tuple-element.101), kind=kOutput, calls=%fused_computation.25 | convolution fusion | flops 1074790400 | bytes 6553600 | tf_op jit(solution)/shard_map/dot_general | solution.py:137
  345.4 1.3 constant_dynamic-slice_fusion
  348.0 41.0 %all_to_all.12 = bf16[8,1,1,2,128,256]{5,4,3,2,1,0:T(8,128)(2,1)S(1)} all-to-all(bf16[8,1,1,2,128,256]{5,4,3,2,1,0:T(8,128)(2,1)S(1)} %copy.42), channel_id=1, replica_groups=mesh['tp'=8,'dp'=8,'hg'=4] {'dp'}, dimensions={0} | all-to-all | bytes 2097152 | tf_op jit(solution)/shard_map/all_to_all | solution.py:149
  388.9 49.5 %reduce-scatter.2.cloned.1.call-done = bf16[32,4096]{1,0:T(8,128)(2,1)} async-done(((bf16[256,4096]{1,0:T(8,128)(2,1)}), bf16[32,4096]{1,0:T(8,128)(2,1)}) %reduce-scatter.2.cloned.1.call-update) | async-done | bytes 262160 | tf_op jit(solution)/shard_map/reduce_scatter | solution.py:136
  438.5 1.7 fusion.27
  (71 shorter events, 15.8 us)
Async XLA Ops:
  7.2 338.0 %copy-start = (s32[8,16]{1,0:T(8,128)S(1)}, s32[8,16]{1,0:T(8,128)}, u32[]{:S(2)}) copy-start(s32[8,16]{1,0:T(8,128)} %param.15) | copy-start | bytes 1540
  7.2 75.2 %all-gather.5.cloned.1.call-start = ((), (), s32[]{:S(2)}) async-start(), calls=%async_computation.2 | async-start | bytes 2359296 | tf_op jit(solution)/shard_map/all_gather | solution.py:101
  7.9 178.6 %all-gather.7.cloned.1.call-start = ((), (), s32[]{:S(2)}) async-start(), calls=%async_computation.3 | async-start | bytes 12976128 | tf_op jit(solution)/shard_map/all_gather | solution.py:103
  8.7 242.7 %all-gather.9.cloned.1.call-start = ((), (), s32[]{:S(2)}) async-start(), calls=%async_computation.4 | async-start | bytes 2621440 | tf_op jit(solution)/shard_map/all_gather | solution.py:120
  82.4 2.2 copy-start.1
  85.3 122.1 %copy-start.6 = (f32[4096]{0:T(1024)S(1)}, f32[4096]{0:T(1024)}, u32[]{:S(2)}) copy-start(f32[4096]{0:T(1024)} %param.10) | copy-start | bytes 49156
  215.1 0.9 copy-start.5
  216.0 4.6 %copy-start.2 = (bf16[1,4,1024,256]{3,2,1,0:T(8,128)(2,1)S(1)}, bf16[1,4,1024,256]{3,2,1,0:T(8,128)(2,1)}, u32[]{:S(2)}) copy-start(bf16[1,4,1024,256]{3,2,1,0:T(8,128)(2,1)} %param.13) | copy-start | bytes 6291460
  218.2 121.5 %all-gather.11.cloned.1.call-start = ((), (), s32[]{:S(2)}) async-start(), calls=%async_computation.5 | async-start | bytes 4325376 | tf_op jit(solution)/shard_map/all_gather | solution.py:134
  218.8 219.7 %reduce-scatter.2.cloned.1.call-start = ((), (), s32[]{:S(2)}) async-start(), calls=%async_computation.6 | async-start | bytes 2359296 | tf_op jit(solution)/shard_map/reduce_scatter | solution.py:136
  220.6 2.5 copy-start.4
  222.9 28.5 %copy-start.7 = (bf16[4,256,128]{2,1,0:T(8,128)(2,1)S(1)}, bf16[4,256,128]{2,1,0:T(8,128)(2,1)}, u32[]{:S(2)}) copy-start(bf16[4,256,128]{2,1,0:T(8,128)(2,1)} %custom-call) | copy-start | bytes 786436
  347.8 90.7 %copy-start.3 = (bf16[1,1,32,4096]{3,2,1,0:T(8,128)(2,1)S(1)}, bf16[1,1,32,4096]{3,2,1,0:T(8,128)(2,1)}, u32[]{:S(2)}) copy-start(bf16[1,1,32,4096]{3,2,1,0:T(8,128)(2,1)} %param.9) | copy-start | bytes 786436
Sparse Core Ops, SparseCore 0:
  10.6 71.7 all-gather.4
  84.2 102.2 all-gather.6
  218.4 32.9 all-gather.8
  252.9 86.7 all-gather.10
  344.7 93.7 reduce-scatter.1
where the time goes:
time: 453 us; the launch traced here: 448 us
  waiting for transfers between devices  308 us (68%)
  local copies, waits for them, and re-layouts  56.2 us (12%)
  blocking collectives  41 us (9%)
  between operations  16.9 us (4%)
  matrix products  16.8 us (4%)
  other arithmetic  9.13 us (2%)
    all_gather x1, waiting for transfers between devices, on_device(): piece = lax.all_gather(qkv_weight, ('dp', 'hg'), axis=0, tiled=True)  101 us
    all_gather x1, waiting for transfers between devices, on_device(): run_rows = lax.all_gather(hidden_in, 'tp', axis=2, tiled=True)[0, 0]  70.9 us
    all_gather x1, waiting for transfers between devices, on_device(): out_full = lax.all_gather(out_weight, ('dp', 'hg'), axis=2, tiled=True)  56 us
    reduce_scatter x1, waiting for transfers between devices, on_device(): lax.psum_scatter(jnp.dot(attended_rows, out_flat, preferred_element_type=...  49.5 us
    all_to_all x1, blocking collectives, on_device(): lax.all_to_all(placed.astype(jnp.bfloat16).reshape(owner_count, group_hea...  41 us
    all_gather x1, waiting for transfers between devices, on_device(): stretch_kv = lax.all_gather(run_kv, 'hg', axis=1, tiled=True)  28 us
    reshape x1, local copies, waits for them, and re-layouts, on_device(): piece.reshape(piece.shape[0], 3 * head_width)  20.9 us
    dynamic_update_slice x4, local copies, waits for them, and re-layouts, one_head(): lax.dynamic_update_slice(head_extended, head_stretch, (length, zero_index))  12.1 us
  transfers between devices with their start and end apart: 5, of which 5 were waited for; matrix products, arithmetic and copies ran while one was open for 10% of the time, Pallas kernels for 0%

commit v1 on v0

v1 whole, which is shorter than its diff:
```python
import functools
import math

import jax
import jax.numpy as jnp
import numpy as np
from jax import lax
from jax.experimental import pallas as pl
from jax.experimental.pallas import tpu as pltpu
from jax.sharding import PartitionSpec as P

ROT = 32
BLOCK = 128
HD = 128
RUN = 256
ROWS = 32
D = 4096
PMAX = 1024
EPS = 1e-05
MESH = pl.DeviceIdType.MESH
BF = jnp.bfloat16
F32 = jnp.float32


def body(
    hid_ref, gain_ref, freq_ref, wq_ref, wo_ref, cache_ref, len_ref, own_ref,
    out_ref, dec_ref,
    abuf, wbuf, acc, tcos, tsin, wobuf, seq, qbuf, qsrc, kvsrc, asrc, atbuf,
    psum, rsum, zsrc, zbuf, fsrc, fbuf, hbuf, dsrc,
    a_ss, a_rs, sw_ss, sw_rs, w_zs, w_xs, w_hs, w_rs, loc,
    o_zs, o_xs, o_zr, o_xr, q_ss, q_rs, k_ss, k_rs, t_ss, t_rs,
    d_ss, d_rs, y_ss, y_rs, z_ss, z_rs, f_ss, f_rs, h_ss, h_rs,
):
    tp = lax.axis_index("tp")
    dp = lax.axis_index("dp")
    x = lax.axis_index("hg")
    y = tp // 2
    zh = tp % 2
    zl = dp // 2
    c = dp % 2

    def dev(x_=x, y_=y, zh_=zh, zl_=zl, c_=c):
        return {"tp": y_ * 2 + zh_, "dp": zl_ * 2 + c_, "hg": x_}

    def rcopy(src, dst, ss, rs, to):
        return pltpu.make_async_remote_copy(
            src_ref=src, dst_ref=dst, send_sem=ss, recv_sem=rs, device_id=to, device_id_type=MESH
        )

    here = dev()
    partner = dev(c_=1 - c)
    xp = dev(x_=(x + 1) % 4)
    xm = dev(x_=(x + 3) % 4)
    x2 = dev(x_=(x + 2) % 4)
    zup = dev(zl_=(zl + 1) % 4)
    zdn = dev(zl_=(zl + 3) % 4)
    zhp = dev(zh_=1 - zh)
    ys = [dev(y_=(y + i) % 4) for i in (1, 3, 2)]

    barrier = pltpu.get_barrier_semaphore()
    peers = [dev(x_=(x + i) % 4, c_=(c + j) % 2) for i in range(4) for j in range(2) if i or j]
    peers += [dev(zl_=(zl + i) % 4, c_=(c + j) % 2) for i in range(1, 4) for j in range(2)]
    peers += ys + [zhp]
    for to in peers:
        pl.semaphore_signal(barrier, inc=1, device_id=to, device_id_type=MESH)

    cache_cp = pltpu.make_async_copy(cache_ref.at[x], seq.at[pl.ds(0, 8)], loc.at[0])
    cache_cp.start()
    wown = wbuf.at[zl, x, pl.ds(c * 128, 128)]
    wcopy = pltpu.make_async_copy(wq_ref.at[c], wown, loc.at[1])
    wcopy.start()
    wocopy = pltpu.make_async_copy(
        wo_ref, wobuf.at[zl, :, pl.ds(pl.multiple_of(x * 128, 128), 128)], loc.at[2]
    )
    wocopy.start()
    rows = hid_ref[...].astype(F32)
    centered = rows - jnp.mean(rows, axis=-1, keepdims=True)
    spread = jnp.mean(centered * centered, axis=-1, keepdims=True)
    arow = lambda r, t: abuf.at[pl.ds(pl.multiple_of(r * RUN + t * ROWS, ROWS), ROWS)]
    abuf[pl.ds(pl.multiple_of(c * RUN + tp * ROWS, ROWS), ROWS), :] = (
        centered * lax.rsqrt(spread + EPS) * gain_ref[...]
    ).astype(BF)
    seq[16] = jnp.zeros((BLOCK, 256), BF)
    pl.semaphore_wait(barrier, len(peers))

    swap = rcopy(wq_ref.at[1 - c], wown, sw_ss, sw_rs, partner)
    swap.start()

    def acopy(r, t, i, to):
        return rcopy(arow(r, t), arow(r, t), a_ss.at[i], a_rs.at[r, t], to)

    a_sent = [acopy(c, tp, 0, zhp), acopy(c, tp, 1, partner)]
    a_sent += [acopy(c, tp, 2 + i, to) for i, to in enumerate(ys)]
    for cp in a_sent:
        cp.start()
    hswap = rcopy(hid_ref, hbuf, h_ss, h_rs, partner)
    hswap.start()

    def order(j):
        m = jnp.where(zl < 2, zl, 3 - zl)
        s = jnp.where((m == 1) & (j < 2), 1 - j, j)
        return jnp.where(zl < 2, s, 3 - s)

    up = lambda s: (s <= zl) & (zl < 3)
    down = lambda s: (s >= zl) & (zl > 0)

    def wz(s, i):
        return rcopy(wbuf.at[s, x], wbuf.at[s, x], w_zs.at[i, s], w_rs.at[s, 0], (zup, zdn)[i])

    def wx(s, i):
        return rcopy(
            wbuf.at[s, x], wbuf.at[s, x], w_xs.at[i, s], w_rs.at[s, 1 + i], (xp, xm)[i]
        )

    def wh(s, i):
        col = (x + 3 - 2 * i) % 4
        half = wbuf.at[s, col, pl.ds(i * 128, 128)]
        return rcopy(half, half, w_hs.at[i, s], w_rs.at[s, 3 + i], (xp, xm)[i])

    def oz(s, i):
        part = wobuf.at[s, :, pl.ds(pl.multiple_of(x * 128, 128), 128)]
        return rcopy(part, part, o_zs.at[i, s], o_zr.at[s], (zup, zdn)[i])

    def ox(s, i):
        part = wobuf.at[s, :, pl.ds(pl.multiple_of(x * 128, 128), 128)]
        return rcopy(part, part, o_xs.at[s, i], o_xr.at[s, i], (xp, xm, x2)[i])

    def relay(make, s):
        @pl.when(up(s))
        def _():
            make(s, 0).start()

        @pl.when(down(s))
        def _():
            make(s, 1).start()

    def step_own(j):
        s = order(j)
        if j:
            wz(s, 0).wait_recv()
        for i in range(2):
            wx(s, i).start()
        relay(wz, s)

    def step_near(j):
        s = order(j)
        for i in range(2):
            wx(s, i).wait_recv()
            wh(s, i).start()

    def project(s, col):
        k = s * 1024 + col * 128
        lhs = jnp.concatenate(
            [
                abuf[:, pl.ds(pl.multiple_of(k, 128), 128)],
                abuf[:, pl.ds(pl.multiple_of(k + 512, 128), 128)],
            ],
            axis=1,
        )
        acc[...] += jnp.dot(lhs, wbuf[s, col], preferred_element_type=F32)

    wcopy.wait()
    swap.wait_recv()
    step_own(0)

    iota = lax.broadcasted_iota(jnp.int32, (RUN, HD), 0)
    for r in range(2):
        pos = (len_ref[zl * 2 + r] + x * RUN + iota).astype(F32) * freq_ref[...]
        tcos[pl.ds(r * RUN, RUN), :] = jnp.cos(pos)
        tsin[pl.ds(r * RUN, RUN), :] = jnp.sin(pos)
    acc[...] = jnp.zeros_like(acc)

    a_fwd = []
    step_near(0)
    for i in range(3):
        t = ((y + (3, 1, 2)[i]) % 4) * 2 + zh
        cp = acopy(c, t, 5 + i, partner)
        cp.wait_recv()
        cp.start()
        a_fwd.append(cp)
    step_own(1)
    t = y * 2 + 1 - zh
    for i, to in enumerate(ys + [partner]):
        cp = acopy(c, t, 8 + i, to)
        if i == 0:
            cp.wait_recv()
        cp.start()
        a_fwd.append(cp)
    step_near(1)
    step_own(2)
    for i in range(3):
        t = ((y + (3, 1, 2)[i]) % 4) * 2 + 1 - zh
        cp = acopy(c, t, 12 + i, partner)
        cp.wait_recv()
        cp.start()
        a_fwd.append(cp)
    step_near(2)
    wocopy.wait()
    relay(oz, zl)
    step_own(3)
    for t in range(8):
        acopy(1 - c, t, 0, partner).wait_recv()

    def early(i, carry):
        j = i // 3
        s = order(j)
        project(s, (x + (i % 3) + 3) % 4)
        return carry

    lax.fori_loop(0, 9, early, 0)
    for j in (1, 2, 3):
        s = order(j)
        oz(s, 0).wait_recv()
        relay(oz, s)
    step_near(3)
    for j in range(4):
        s = order(j)
        for i in range(2):
            if j < 2:
                ox(s, i).start()
    for j in range(3):
        for i in range(2):
            wh_in = wbuf.at[order(j), (x + 2) % 4, pl.ds(i * 128, 128)]
            rcopy(wh_in, wh_in, w_hs.at[i, 0], w_rs.at[order(j), 3 + i], xp).wait_recv()

    def late(i, carry):
        s = order(jnp.where(i < 3, i, 3))
        project(s, jnp.where(i < 3, (x + 2) % 4, (x + i) % 4))
        return carry

    lax.fori_loop(0, 3, late, 0)
    lax.fori_loop(0, 3, lambda i, carry: (project(order(3), (x + i + 3) % 4), carry)[1], 0)
    for i in range(2):
        wh_in = wbuf.at[order(3), (x + 2) % 4, pl.ds(i * 128, 128)]
        rcopy(wh_in, wh_in, w_hs.at[i, 0], w_rs.at[order(3), 3 + i], xp).wait_recv()
    project(order(3), (x + 2) % 4)

    lane = lax.broadcasted_iota(jnp.int32, (RUN, HD), 1)

    def qcopies(h, r):
        to = dev(x_=2 * c + h, c_=r)
        i = h * 2 + r
        kdst = seq.at[pl.ds(8 + x * 2, 2)]
        return (
            rcopy(qsrc.at[h, r], qbuf.at[x], q_ss.at[i], q_rs.at[x], to),
            rcopy(kvsrc.at[h, r], kdst, k_ss.at[i], k_rs.at[x], to),
            pltpu.make_async_copy(qsrc.at[h, r], qbuf.at[x], q_rs.at[x]),
            pltpu.make_async_copy(kvsrc.at[h, r], kdst, k_rs.at[x]),
        )

    for r in range(2):
        sl = pl.ds(r * RUN, RUN)
        cos = tcos[sl, :]
        sin = tsin[sl, :]
        sin_a = jnp.where(lane < 16, -sin, 0.0)
        sin_b = jnp.where(lane < 16, 0.0, sin)

        def turn(v):
            return v * cos + pltpu.roll(v, HD - 16, 1) * sin_a + pltpu.roll(v, 16, 1) * sin_b

        for h in range(2):
            piece = lambda i: acc[sl, pl.ds((i * 2 + h) * HD, HD)]
            qsrc[h, r] = turn(piece(0)).astype(BF)
            kvsrc[h, r, :, :, pl.ds(0, HD)] = turn(piece(1)).astype(BF).reshape(2, BLOCK, HD)
            kvsrc[h, r, :, :, pl.ds(HD, HD)] = piece(2).astype(BF).reshape(2, BLOCK, HD)
            mine = (x == 2 * c + h) & (c == r)

            @pl.when(jnp.logical_not(mine))
            def _():
                cps = qcopies(h, r)
                cps[1].start()
                cps[0].start()

            @pl.when(mine)
            def _():
                cps = qcopies(h, r)
                cps[3].start()
                cps[2].start()

    length = len_ref[dp]
    cached = length // BLOCK
    valid_end = cached + 8
    owner = [own_ref[dp, b] for b in range(16)]
    rank = []
    for b in range(16):
        n = jnp.int32(0)
        for e in range(b):
            n += jnp.where((owner[e] == owner[b]) & (e < valid_end), 1, 0)
        rank.append(n)
    code = [
        jnp.where(b < valid_end, owner[b] * 2 + rank[b], -1) for b in range(16)
    ]
    source = [jnp.where(b < cached, b, 8 + b - cached) for b in range(16)]
    slots = []
    for s in range(16):
        n = jnp.int32(16)
        for b in range(16):
            n = jnp.where(code[b] == s, source[b], n)
        slots.append(n)

    cache_cp.wait()
    for i in range(4):
        pltpu.make_async_copy(qsrc.at[0, 0], qbuf.at[i], q_rs.at[i]).wait()
        pltpu.make_async_copy(
            kvsrc.at[0, 0], seq.at[pl.ds(8 + i * 2, 2)], k_rs.at[i]
        ).wait()

    def dcopies(o):
        to = {"tp": tp, "dp": o, "hg": x}
        return (
            rcopy(dsrc.at[o], dec_ref.at[dp], d_ss.at[o], d_rs.at[dp], to),
            pltpu.make_async_copy(dsrc.at[o], dec_ref.at[dp], d_rs.at[dp]),
        )

    for o in range(8):
        for k in range(2):
            dsrc[o, k] = seq[slots[o * 2 + k]]

        @pl.when(o != dp)
        def _():
            dcopies(o)[0].start()

        @pl.when(o == dp)
        def _():
            dcopies(o)[1].start()

    for j in range(4):
        s = order(j)
        for i in range(3):
            if j >= 2 or i == 2:
                ox(s, i).start()

    scale = 1.0 / math.sqrt(HD)

    def tcopies(g, k):
        to = dev(x_=g, c_=k)
        dst = atbuf.at[c, x]
        return (
            rcopy(asrc.at[g], dst, t_ss.at[g, k], t_rs.at[c, x], to),
            pltpu.make_async_copy(asrc.at[g], dst, t_rs.at[c, x]),
        )

    for g in (3, 2, 1, 0):
        n = PMAX + (g + 1) * RUN
        scores = (
            lax.dot_general(
                qbuf[g], seq[0 : n // BLOCK, :, 0:HD].reshape(n, HD), (((1,), (1,)), ((), ())),
                preferred_element_type=F32,
            )
            * scale
        )
        col = lax.broadcasted_iota(jnp.int32, (RUN, n), 1)
        row = lax.broadcasted_iota(jnp.int32, (RUN, n), 0)
        keep = (col < length) | ((col >= PMAX) & (col <= row + (PMAX + g * RUN)))
        scores = jnp.where(keep, scores, -jnp.inf)
        top = jnp.max(scores, axis=1, keepdims=True)
        weights = jnp.exp(scores - top)
        total = jnp.sum(weights, axis=1, keepdims=True)
        asrc[g] = (
            jnp.dot(
                weights.astype(BF),
                seq[0 : n // BLOCK, :, HD : 2 * HD].reshape(n, HD),
                preferred_element_type=F32,
            )
            / total
        ).astype(BF)
        for k in range(2):
            mine = (x == g) & (c == k)

            @pl.when(jnp.logical_not(mine))
            def _():
                tcopies(g, k)[0].start()

            @pl.when(mine)
            def _():
                tcopies(g, k)[1].start()

    for r in range(2):
        for h in range(4):
            pltpu.make_async_copy(asrc.at[0], atbuf.at[r, h], t_rs.at[r, h]).wait()
    lhs = jnp.concatenate(
        [jnp.concatenate([atbuf[r, h] for h in range(4)], axis=1) for r in range(2)], axis=0
    )

    def ycopy(q, i):
        to = (y + (1, 3, 2)[i]) % 4
        return rcopy(psum.at[q, to], rsum.at[q, i], y_ss.at[q, i], y_rs.at[q, i], ys[i])

    def zcopy(q):
        return rcopy(zsrc.at[q], zbuf.at[q], z_ss.at[q], z_rs.at[q], zhp)

    def fcopy(q):
        return rcopy(fsrc.at[q], fbuf.at[q], f_ss.at[q], f_rs.at[q], partner)

    for q in range(4):
        s = order(q)
        for i in range(3):
            ox(s, i).wait_recv()
        part = jnp.dot(lhs, wobuf[s], preferred_element_type=F32).astype(BF)
        for to in range(4):
            for r in range(2):
                psum[q, to, r] = part[r * RUN + to * 64 : r * RUN + to * 64 + 64]
        for i in (2, 0, 1):
            ycopy(q, i).start()
    sums = []
    for q in range(4):
        for i in range(3):
            ycopy(q, i).wait_recv()
        for r in range(2):
            far = pl.ds(pl.multiple_of((1 - zh) * ROWS, ROWS), ROWS)
            total = psum[q, y, r, far, :].astype(F32)
            for i in range(3):
                total += rsum[q, i, r, far, :].astype(F32)
            zsrc[q, r] = total.astype(BF)
        zcopy(q).start()
    near = pl.ds(pl.multiple_of(zh * ROWS, ROWS), ROWS)

    def total_of(q, r):
        total = psum[q, y, r, near, :].astype(F32)
        for i in range(3):
            total += rsum[q, i, r, near, :].astype(F32)
        return total + zbuf[q, r].astype(F32)

    for q in range(4):
        zcopy(q).wait_recv()
        if q == 0:
            hswap.wait_recv()
        cols = pl.ds(pl.multiple_of(order(q) * 1024 + c * 512, 512), 512)
        fsrc[q] = (hbuf[:, cols].astype(F32) + total_of(q, 1 - c)).astype(BF)
        fcopy(q).start()
        out_ref[:, cols] = (hid_ref[:, cols].astype(F32) + total_of(q, c)).astype(BF)
    for q in range(4):
        fcopy(q).wait_recv()
        cols = pl.ds(pl.multiple_of(order(q) * 1024 + (1 - c) * 512, 512), 512)
        out_ref[:, cols] = fbuf[q]

    for i in range(8):
        pltpu.make_async_copy(dsrc.at[0], dec_ref.at[i], d_rs.at[i]).wait()
    swap.wait_send()
    hswap.wait_send()
    for cp in a_sent + a_fwd:
        cp.wait_send()
    for j in range(4):
        for make in (wz, oz):

            @pl.when(up(j))
            def _():
                make(j, 0).wait_send()

            @pl.when(down(j))
            def _():
                make(j, 1).wait_send()

        for i in range(2):
            wx(j, i).wait_send()
            wh(j, i).wait_send()
        for i in range(3):
            ox(j, i).wait_send()
            ycopy(j, i).wait_send()
        zcopy(j).wait_send()
        fcopy(j).wait_send()
    for h in range(2):
        for r in range(2):

            @pl.when(jnp.logical_not((x == 2 * c + h) & (c == r)))
            def _():
                cps = qcopies(h, r)
                cps[0].wait_send()
                cps[1].wait_send()

    for g in range(4):
        for k in range(2):

            @pl.when(jnp.logical_not((x == g) & (c == k)))
            def _():
                tcopies(g, k)[0].wait_send()

    for o in range(8):

        @pl.when(o != dp)
        def _():
            dcopies(o)[0].wait_send()


def on_device(hidden_in, norm_gain, qkv_weight, out_weight, cache_kv, cached_lengths, owner_table):
    hid = hidden_in.reshape(ROWS, D)
    wq = (
        qkv_weight.reshape(128, 3, 2, 2, HD).transpose(2, 0, 1, 3, 4).reshape(2, 128, 6 * HD)
    )
    wo = out_weight.reshape(4 * HD, 128)
    cache = cache_kv.reshape(4, PMAX // BLOCK, BLOCK, 2 * HD)
    half = 10000.0 ** (-2.0 * np.arange(ROT // 2) / ROT)
    freq = np.zeros((1, HD), np.float32)
    freq[0, :ROT] = np.concatenate([half, half])
    vm = pl.BlockSpec(memory_space=pltpu.VMEM)
    sm = pl.BlockSpec(memory_space=pltpu.SMEM)
    hbm = pl.BlockSpec(memory_space=pl.ANY)
    dma = pltpu.SemaphoreType.DMA
    scratch = [
        pltpu.VMEM((512, D), BF),
        pltpu.VMEM((4, 4, 256, 768), BF),
        pltpu.VMEM((512, 768), F32),
        pltpu.VMEM((512, HD), F32),
        pltpu.VMEM((512, HD), F32),
        pltpu.VMEM((4, 512, 512), BF),
        pltpu.VMEM((17, BLOCK, 256), BF),
        pltpu.VMEM((4, RUN, HD), BF),
        pltpu.VMEM((2, 2, RUN, HD), BF),
        pltpu.VMEM((2, 2, 2, BLOCK, 2 * HD), BF),
        pltpu.VMEM((4, RUN, HD), BF),
        pltpu.VMEM((2, 4, RUN, HD), BF),
        pltpu.VMEM((4, 4, 2, 64, 512), BF),
        pltpu.VMEM((4, 3, 2, 64, 512), BF),
        pltpu.VMEM((4, 2, ROWS, 512), BF),
        pltpu.VMEM((4, 2, ROWS, 512), BF),
        pltpu.VMEM((4, ROWS, 512), BF),
        pltpu.VMEM((4, ROWS, 512), BF),
        pltpu.VMEM((ROWS, D), BF),
        pltpu.VMEM((8, 2, BLOCK, 256), BF),
        dma((15,)), dma((2, 8)), dma, dma, dma((2, 4)), dma((2, 4)), dma((2, 4)), dma((4, 5)),
        dma((3,)),
        dma((2, 4)), dma((4, 3)), dma((4,)), dma((4, 3)),
        dma((4,)), dma((4,)), dma((4,)), dma((4,)), dma((4, 2)), dma((2, 4)),
        dma((8,)), dma((8,)), dma((4, 3)), dma((4, 3)), dma((4,)), dma((4,)),
        dma((4,)), dma((4,)), dma, dma,
    ]
    out, dec = pl.pallas_call(
        body,
        name="branch",
        out_shape=(
            jax.ShapeDtypeStruct((ROWS, D), BF),
            jax.ShapeDtypeStruct((8, 2, BLOCK, 2 * HD), BF),
        ),
        in_specs=[vm, vm, vm, vm, vm, hbm, sm, sm],
        out_specs=(vm, hbm),
        scratch_shapes=scratch,
        compiler_params=pltpu.CompilerParams(
            collective_id=0, has_side_effects=True, vmem_limit_bytes=60 * 1024 * 1024
        ),
    )(hid, norm_gain.reshape(1, D), jnp.asarray(freq), wq, wo, cache, cached_lengths, owner_table)
    return out.reshape(hidden_in.shape), dec.reshape(1, 1, 8, 2, BLOCK, 2 * HD)


def solution(mesh):
    return jax.shard_map(
        on_device,
        mesh=mesh,
        in_specs=(
            P("dp", "hg", "tp", None),
            P(),
            P(("dp", "hg"), None, "tp", None),
            P("tp", None, ("dp", "hg")),
            P("dp", "tp", None, None),
            P(),
            P(),
        ),
        out_specs=(P("dp", "hg", "tp", None), P("dp", ("tp", "hg"), None, None, None, None)),
        check_vma=False,
    )
```

time: 453 us -> 176 us (0.39); the launches traced: 448 us -> 176 us
  waiting for transfers between devices: 308 us -> 0 us
  Pallas kernels: 0 us -> 169 us
  local copies, waits for them, and re-layouts: 56.2 us -> 6.15 us
  blocking collectives: 41 us -> 0 us
  matrix products: 16.8 us -> 0 us
  between operations: 16.9 us -> 0.64 us
  other arithmetic: 9.13 us -> 0 us
    all_gather x4 -> x0, waiting for transfers between devices: 256 us -> none  [the longest x1 101 us: on_device(): piece = lax.all_gather(qkv_weight, ('dp', 'hg'), axis=0, tiled=True)]
    pallas_call x0 -> x1, Pallas kernels: none -> 169 us  [on_device(): pl.pallas_call(body, name='branch', out_shape=(jax.ShapeDtypeStruct((ROWS...]
    reduce_scatter x1 -> x0, waiting for transfers between devices: 49.5 us -> none  [on_device(): lax.psum_scatter(jnp.dot(attended_rows, out_flat, preferred_element_type=...]
    all_to_all x1 -> x0, blocking collectives: 41 us -> none  [on_device(): lax.all_to_all(placed.astype(jnp.bfloat16).reshape(owner_count, group_hea...]
    reshape x4 -> x2, local copies, waits for them, and re-layouts: 21.5 us -> 2.2 us  [on_device(): qkv_weight.reshape(128, 3, 2, 2, HD).transpose(2, 0, 1, 3, 4)]
    dot_general x11 -> x0, matrix products: 16.8 us -> none  [the longest x1 6.91 us: on_device(): jnp.dot(normed, piece.reshape(piece.shape[0], 3 * head_width), preferred_...]
    dynamic_update_slice x8 -> x0, local copies, waits for them, and re-layouts: 16.4 us -> none  [the longest x4 12.1 us: one_head(): lax.dynamic_update_slice(head_extended, head_stretch, (length, zero_index))]
    squeeze x8 -> x0, local copies, waits for them, and re-layouts: 9.53 us -> none  [on_device(): lax.map(one_head, (queries.transpose(1, 0, 2), extended, stretch_kv))]
  transfers between devices with their start and end apart: 5 -> 0, of which waited for: 5 -> 0; matrix products, arithmetic and copies ran while one was open for 10% -> 0% of each run, Pallas kernels for 0% -> 0%
where the time goes in v1:
time: 176 us
  Pallas kernels  169 us (96%)
  local copies, waits for them, and re-layouts  6.15 us (3%)
    pallas_call x1, Pallas kernels, on_device(): pl.pallas_call(body, name='branch', out_shape=(jax.ShapeDtypeStruct((ROWS...  169 us
    unnamed x2, local copies, waits for them, and re-layouts  3.96 us

profile of v1, /device:TPU:3, one launch (start us, length us, event | category | flops | bytes accessed | tf_op | source)
XLA Modules:
  0.0 176.0 jit_solution(4563146460728088078)
XLA Ops:
  0.6 1.3 copy.12
  1.9 0.9 reshape.31.wq_ref
  2.8 169.2 %branch.1 = (bf16[32,4096]{1,0:T(8,128)(2,1)}, bf16[8,2,128,256]{3,2,1,0:T(8,128)(2,1)}) custom-call(bf16[32,4096]{1,0:T(8,128)(2,1)} %bitcast.15, f32[1,4096]{1,0:T(1,128)} %bitcast.17, f32[1,128]{1,0:T(1,128)} %constant.2.clone.freq_ref, bf16[2,128,768]{2,1,0:T(8,128)(2,1)} %reshape.31.wq_ref, bf16[512,128]{1,0:T(8,128)(2,1)} %bitcast.16, ...), custom_call_target="tpu_custom_call" | custom-call | tf_op jit(solution)/shard_map/branch/pallas_call | solution.py:527
  172.0 1.7 copy.15
  173.7 2.3 %copy.16 = bf16[1,1,8,2,128,256]{5,4,3,2,1,0:T(8,128)(2,1)} copy(bf16[1,1,8,2,128,256]{5,4,3,2,1,0:T(8,128)(2,1)} %bitcast.12) | data formatting | bytes 2097152

commit v2 on v1

--- a/solution.py
+++ b/solution.py
@@ -26,10 +26,10 @@
     hid_ref, gain_ref, freq_ref, wq_ref, wo_ref, cache_ref, len_ref, own_ref,
     out_ref, dec_ref,
     abuf, wbuf, acc, tcos, tsin, wobuf, seq, qbuf, qsrc, kvsrc, asrc, atbuf,
-    psum, rsum, zsrc, zbuf, fsrc, fbuf, hbuf, dsrc,
+    psum, rbuf, rsrc, zsrc, zbuf, fsrc, fbuf, dsrc,
     a_ss, a_rs, sw_ss, sw_rs, w_zs, w_xs, w_hs, w_rs, loc,
     o_zs, o_xs, o_zr, o_xr, q_ss, q_rs, k_ss, k_rs, t_ss, t_rs,
-    d_ss, d_rs, y_ss, y_rs, z_ss, z_rs, f_ss, f_rs, h_ss, h_rs,
+    d_ss, d_rs, y_ss, y_rs, z_ss, z_rs, f_ss, f_rs,
 ):
     tp = lax.axis_index("tp")
     dp = lax.axis_index("dp")
@@ -55,12 +55,13 @@
     zup = dev(zl_=(zl + 1) % 4)
     zdn = dev(zl_=(zl + 3) % 4)
     zhp = dev(zh_=1 - zh)
+    zhq = dev(zh_=1 - zh, c_=1 - c)
     ys = [dev(y_=(y + i) % 4) for i in (1, 3, 2)]
 
     barrier = pltpu.get_barrier_semaphore()
     peers = [dev(x_=(x + i) % 4, c_=(c + j) % 2) for i in range(4) for j in range(2) if i or j]
     peers += [dev(zl_=(zl + i) % 4, c_=(c + j) % 2) for i in range(1, 4) for j in range(2)]
-    peers += ys + [zhp]
+    peers += ys + [zhp, zhq]
     for to in peers:
         pl.semaphore_signal(barrier, inc=1, device_id=to, device_id_type=MESH)
 
@@ -93,8 +94,6 @@
     a_sent += [acopy(c, tp, 2 + i, to) for i, to in enumerate(ys)]
     for cp in a_sent:
         cp.start()
-    hswap = rcopy(hid_ref, hbuf, h_ss, h_rs, partner)
-    hswap.start()
 
     def order(j):
         m = jnp.where(zl < 2, zl, 3 - zl)
@@ -118,12 +117,11 @@
         return rcopy(half, half, w_hs.at[i, s], w_rs.at[s, 3 + i], (xp, xm)[i])
 
     def oz(s, i):
-        part = wobuf.at[s, :, pl.ds(pl.multiple_of(x * 128, 128), 128)]
-        return rcopy(part, part, o_zs.at[i, s], o_zr.at[s], (zup, zdn)[i])
-
-    def ox(s, i):
-        part = wobuf.at[s, :, pl.ds(pl.multiple_of(x * 128, 128), 128)]
-        return rcopy(part, part, o_xs.at[s, i], o_xr.at[s, i], (xp, xm, x2)[i])
+        return rcopy(wobuf.at[s], wobuf.at[s], o_zs.at[i, s], o_zr.at[s], (zup, zdn)[i])
+
+    def ox(i):
+        part = wobuf.at[zl, :, pl.ds(pl.multiple_of(x * 128, 128), 128)]
+        return rcopy(wo_ref, part, o_xs.at[i], o_xr.at[i], (xp, xm, x2)[i])
 
     def relay(make, s):
         @pl.when(up(s))
@@ -162,6 +160,8 @@
     wcopy.wait()
     swap.wait_recv()
     step_own(0)
+    for i in range(3):
+        ox(i).start()
 
     iota = lax.broadcasted_iota(jnp.int32, (RUN, HD), 0)
     for r in range(2):
@@ -195,9 +195,11 @@
         cp.start()
         a_fwd.append(cp)
     step_near(2)
+    step_own(3)
     wocopy.wait()
+    for i in range(3):
+        ox(i).wait_recv()
     relay(oz, zl)
-    step_own(3)
     for t in range(8):
         acopy(1 - c, t, 0, partner).wait_recv()
 
@@ -208,16 +210,15 @@
         return carry
 
     lax.fori_loop(0, 9, early, 0)
-    for j in (1, 2, 3):
-        s = order(j)
-        oz(s, 0).wait_recv()
-        relay(oz, s)
+    middle = (zl == 1) | (zl == 2)
+
+    @pl.when(middle)
+    def _():
+        for j in (1, 2):
+            oz(order(j), 0).wait_recv()
+            relay(oz, order(j))
+
     step_near(3)
-    for j in range(4):
-        s = order(j)
-        for i in range(2):
-            if j < 2:
-                ox(s, i).start()
     for j in range(3):
         for i in range(2):
             wh_in = wbuf.at[order(j), (x + 2) % 4, pl.ds(i * 128, 128)]
@@ -276,6 +277,11 @@
                 cps = qcopies(h, r)
                 cps[3].start()
                 cps[2].start()
+
+    @pl.when(middle)
+    def _():
+        oz(order(3), 0).wait_recv()
+        relay(oz, order(3))
 
     length = len_ref[dp]
     cached = length // BLOCK
@@ -324,12 +330,6 @@
         def _():
             dcopies(o)[1].start()
 
-    for j in range(4):
-        s = order(j)
-        for i in range(3):
-            if j >= 2 or i == 2:
-                ox(s, i).start()
-
     scale = 1.0 / math.sqrt(HD)
 
     def tcopies(g, k):
@@ -382,62 +382,88 @@
         [jnp.concatenate([atbuf[r, h] for h in range(4)], axis=1) for r in range(2)], axis=0
     )
 
+    yp = (y + 1) % 4
+    ym = (y + 3) % 4
+    yf = (y + 2) % 4
+
     def ycopy(q, i):
-        to = (y + (1, 3, 2)[i]) % 4
-        return rcopy(psum.at[q, to], rsum.at[q, i], y_ss.at[q, i], y_rs.at[q, i], ys[i])
-
-    def zcopy(q):
-        return rcopy(zsrc.at[q], zbuf.at[q], z_ss.at[q], z_rs.at[q], zhp)
+        src = (
+            psum.at[q, yf, 0], psum.at[q, yf, 1], psum.at[q, yp, 1], psum.at[q, ym, 0],
+            rsrc.at[q, 0], rsrc.at[q, 1],
+        )[i]
+        return rcopy(src, rbuf.at[q, i], y_ss.at[q, i], y_rs.at[q, i], ys[i % 2])
+
+    def zcopy(q, r):
+        to = dev(zh_=1 - zh, c_=r)
+        return rcopy(zsrc.at[q, r], zbuf.at[q, c], z_ss.at[q, r], z_rs.at[q, c], to)
 
     def fcopy(q):
         return rcopy(fsrc.at[q], fbuf.at[q], f_ss.at[q], f_rs.at[q], partner)
 
+    def add_far(q):
+        for i, to in enumerate((yp, ym)):
+            ycopy(q, i).wait_recv()
+            rsrc[q, i] = (psum[q, to, i].astype(F32) + rbuf[q, i].astype(F32)).astype(BF)
+            ycopy(q, 4 + i).start()
+
     for q in range(4):
         s = order(q)
-        for i in range(3):
-            ox(s, i).wait_recv()
+        if q:
+
+            @pl.when(jnp.logical_not(middle))
+            def _():
+                oz(s, 0).wait_recv()
+
         part = jnp.dot(lhs, wobuf[s], preferred_element_type=F32).astype(BF)
-        for to in range(4):
-            for r in range(2):
-                psum[q, to, r] = part[r * RUN + to * 64 : r * RUN + to * 64 + 64]
-        for i in (2, 0, 1):
+        for i in range(2):
+            for to in range(4):
+                for r in range(2):
+                    psum[q, to, i, r] = part[
+                        r * RUN + to * 64 : r * RUN + to * 64 + 64, i * 256 : i * 256 + 256
+                    ]
+        for i in range(4):
             ycopy(q, i).start()
-    sums = []
+        if q > 1:
+            add_far(q - 2)
+    for q in (2, 3):
+        add_far(q)
+    far = pl.ds(pl.multiple_of((1 - zh) * ROWS, ROWS), ROWS)
+    near = pl.ds(pl.multiple_of(zh * ROWS, ROWS), ROWS)
+
+    def total_of(q, r, rows):
+        a, b = (
+            psum[q, y, i, r, rows, :].astype(F32)
+            + rbuf[q, 3 - i, r, rows, :].astype(F32)
+            + rbuf[q, 4 + i, r, rows, :].astype(F32)
+            for i in range(2)
+        )
+        return jnp.concatenate([a, b], axis=1)
+
     for q in range(4):
-        for i in range(3):
+        for i in range(2, 6):
             ycopy(q, i).wait_recv()
         for r in range(2):
-            far = pl.ds(pl.multiple_of((1 - zh) * ROWS, ROWS), ROWS)
-            total = psum[q, y, r, far, :].astype(F32)
-            for i in range(3):
-                total += rsum[q, i, r, far, :].astype(F32)
-            zsrc[q, r] = total.astype(BF)
-        zcopy(q).start()
-    near = pl.ds(pl.multiple_of(zh * ROWS, ROWS), ROWS)
-
-    def total_of(q, r):
-        total = psum[q, y, r, near, :].astype(F32)
-        for i in range(3):
-            total += rsum[q, i, r, near, :].astype(F32)
-        return total + zbuf[q, r].astype(F32)
-
-    for q in range(4):
-        zcopy(q).wait_recv()
-        if q == 0:
-            hswap.wait_recv()
-        cols = pl.ds(pl.multiple_of(order(q) * 1024 + c * 512, 512), 512)
-        fsrc[q] = (hbuf[:, cols].astype(F32) + total_of(q, 1 - c)).astype(BF)
+            zsrc[q, r] = total_of(q, r, far).astype(BF)
+            zcopy(q, r).start()
+        fsrc[q] = total_of(q, 1 - c, near).astype(BF)
         fcopy(q).start()
-        out_ref[:, cols] = (hid_ref[:, cols].astype(F32) + total_of(q, c)).astype(BF)
     for q in range(4):
         fcopy(q).wait_recv()
-        cols = pl.ds(pl.multiple_of(order(q) * 1024 + (1 - c) * 512, 512), 512)
-        out_ref[:, cols] = fbuf[q]
+        for k in range(2):
+            pltpu.make_async_copy(zsrc.at[0, 0], zbuf.at[q, k], z_rs.at[q, k]).wait()
+        base = order(q) * 1024
+        cols = pl.ds(pl.multiple_of(base + c * 512, 512), 512)
+        total = total_of(q, c, near) + zbuf[q, c].astype(F32)
+        out_ref[:, cols] = (hid_ref[:, cols].astype(F32) + total).astype(BF)
+        cols = pl.ds(pl.multiple_of(base + (1 - c) * 512, 512), 512)
+        total = fbuf[q].astype(F32) + zbuf[q, 1 - c].astype(F32)
+        out_ref[:, cols] = (hid_ref[:, cols].astype(F32) + total).astype(BF)
 
     for i in range(8):
         pltpu.make_async_copy(dsrc.at[0], dec_ref.at[i], d_rs.at[i]).wait()
     swap.wait_send()
-    hswap.wait_send()
+    for i in range(3):
+        ox(i).wait_send()
     for cp in a_sent + a_fwd:
         cp.wait_send()
     for j in range(4):
@@ -454,10 +480,10 @@
         for i in range(2):
             wx(j, i).wait_send()
             wh(j, i).wait_send()
-        for i in range(3):
-            ox(j, i).wait_send()
+        for i in range(6):
             ycopy(j, i).wait_send()
-        zcopy(j).wait_send()
+        for r in range(2):
+            zcopy(j, r).wait_send()
         fcopy(j).wait_send()
     for h in range(2):
         for r in range(2):
@@ -509,20 +535,20 @@
         pltpu.VMEM((2, 2, 2, BLOCK, 2 * HD), BF),
         pltpu.VMEM((4, RUN, HD), BF),
         pltpu.VMEM((2, 4, RUN, HD), BF),
-        pltpu.VMEM((4, 4, 2, 64, 512), BF),
-        pltpu.VMEM((4, 3, 2, 64, 512), BF),
+        pltpu.VMEM((4, 4, 2, 2, 64, 256), BF),
+        pltpu.VMEM((4, 6, 2, 64, 256), BF),
+        pltpu.VMEM((4, 2, 2, 64, 256), BF),
         pltpu.VMEM((4, 2, ROWS, 512), BF),
         pltpu.VMEM((4, 2, ROWS, 512), BF),
         pltpu.VMEM((4, ROWS, 512), BF),
         pltpu.VMEM((4, ROWS, 512), BF),
-        pltpu.VMEM((ROWS, D), BF),
         pltpu.VMEM((8, 2, BLOCK, 256), BF),
         dma((15,)), dma((2, 8)), dma, dma, dma((2, 4)), dma((2, 4)), dma((2, 4)), dma((4, 5)),
         dma((3,)),
-        dma((2, 4)), dma((4, 3)), dma((4,)), dma((4, 3)),
+        dma((2, 4)), dma((3,)), dma((4,)), dma((3,)),
         dma((4,)), dma((4,)), dma((4,)), dma((4,)), dma((4, 2)), dma((2, 4)),
-        dma((8,)), dma((8,)), dma((4, 3)), dma((4, 3)), dma((4,)), dma((4,)),
-        dma((4,)), dma((4,)), dma, dma,
+        dma((8,)), dma((8,)), dma((4, 6)), dma((4, 6)), dma((4, 2)), dma((4, 2)),
+        dma((4,)), dma((4,)),
     ]
     out, dec = pl.pallas_call(
         body,

time: 176 us -> 151 us (0.86)
  Pallas kernels: 169 us -> 144 us
    pallas_call x1, Pallas kernels: 169 us -> 144 us  [on_device(): pl.pallas_call(body, name='branch', out_shape=(jax.ShapeDtypeStruct((ROWS...]
where the time goes in v2:
time: 151 us
  Pallas kernels  144 us (95%)
  local copies, waits for them, and re-layouts  6.15 us (4%)
    pallas_call x1, Pallas kernels, on_device(): pl.pallas_call(body, name='branch', out_shape=(jax.ShapeDtypeStruct((ROWS...  144 us
    unnamed x2, local copies, waits for them, and re-layouts  3.96 us

profile of v2, /device:TPU:3, one launch (start us, length us, event | category | flops | bytes accessed | tf_op | source)
XLA Modules:
  0.0 150.8 jit_solution(18339454931055403936)
XLA Ops:
  0.6 1.3 copy.12
  1.9 0.9 reshape.31.wq_ref
  2.8 144.0 %branch.1 = (bf16[32,4096]{1,0:T(8,128)(2,1)}, bf16[8,2,128,256]{3,2,1,0:T(8,128)(2,1)}) custom-call(bf16[32,4096]{1,0:T(8,128)(2,1)} %bitcast.15, f32[1,4096]{1,0:T(1,128)} %bitcast.17, f32[1,128]{1,0:T(1,128)} %constant.2.clone.freq_ref, bf16[2,128,768]{2,1,0:T(8,128)(2,1)} %reshape.31.wq_ref, bf16[512,128]{1,0:T(8,128)(2,1)} %bitcast.16, ...), custom_call_target="tpu_custom_call" | custom-call | tf_op jit(solution)/shard_map/branch/pallas_call | solution.py:553
  146.9 1.7 %copy.15 = bf16[1,1,32,4096]{3,2,1,0:T(8,128)(2,1)} copy(bf16[1,1,32,4096]{3,2,1,0:T(8,128)(2,1)} %bitcast.14) | data formatting | bytes 524288
  148.5 2.3 %copy.16 = bf16[1,1,8,2,128,256]{5,4,3,2,1,0:T(8,128)(2,1)} copy(bf16[1,1,8,2,128,256]{5,4,3,2,1,0:T(8,128)(2,1)} %bitcast.12) | data formatting | bytes 2097152
